TPU v7x, 128 devices: a whole 4x4x4 slice. The times are simulated.
128 devices in a mesh: ctx: 16 (over z, y), head: 8 (over x, core).
Axes of the slice: x: 4, y: 4, z: 4, core: 2. Of those that a mesh axis runs over, the one named last changes fastest.
Arguments:
- query_states: bfloat16 [16384, 128, 128], P(('ctx', 'head')), may hold values from -8 to 8
- key_states: bfloat16 [16384, 8, 128], P(('ctx', 'head')), may hold values from -8 to 8
- value_states: bfloat16 [16384, 8, 128], P(('ctx', 'head')), may hold values from -6 to 6
- slash_offsets: int32 [8, 256, 12], P('head'), may hold values from 0 to 31, as said below
- slash_counts: int32 [8, 256], P('head'), may hold values from 1 to 12, as said below
- vertical_blocks: int32 [8, 256, 12], P('head'), may hold values from 0 to 223, as said below
- vertical_counts: int32 [8, 256], P('head'), may hold values from 0 to 12, as said below
Outputs:
- attended: bfloat16 [16384, 128, 128], P(('ctx', 'head'))
Inputs may be any that keep to these rules, and one draw needn't show every extreme that they name: `slash_offsets`: for every head and query block b, the entries j < slash_counts are distinct, at most b and below 32; entry 0 is 0; the other entries are 0. `slash_counts`: at most min(12, b + 1) for query block b. `vertical_blocks`: for every head and query block b, the entries j < vertical_counts are distinct blocks at most b - 32; the other entries are 0. `vertical_counts`: at most max(0, b - 31) for query block b.
All inputs are finite; a program needn't handle non-finite values.
Results may differ from a plain program's by a relative error of at most 0.0049.
Values may be sent and summed in bfloat16 or wider, within the bound.
A program may use at most 128 MiB of HBM per device.

v0:
```python
import jax
import jax.numpy as jnp
from jax import lax
from jax.sharding import PartitionSpec as P

BLK = 64
G = 16
NEG = -1e30


def visit(carry_state, query_group, key_table, value_table, query_ids, blocks, live_slots):
    maxima, totals, running = carry_state
    group_count, block_len, local_groups, group_heads, head_dim = query_group.shape
    head_lanes = jnp.arange(local_groups, dtype=jnp.int32)[None, :, None]
    key_tiles = key_table[blocks, :, head_lanes].reshape(
        group_count, local_groups, 2 * block_len, head_dim
    )
    value_tiles = value_table[blocks, :, head_lanes].reshape(
        group_count, local_groups, 2 * block_len, head_dim
    )
    scores = jnp.einsum(
        "bqngd,bnsd->bngqs", query_group, key_tiles, preferred_element_type=jnp.float32
    ) * head_dim ** (-0.5)
    within = jnp.arange(block_len, dtype=jnp.int32)
    key_pos = (blocks[..., None] * block_len + within).reshape(
        group_count, local_groups, 2 * block_len
    )
    key_live = jnp.repeat(live_slots, block_len, axis=2)
    query_pos = query_ids[:, None] * block_len + within
    visible = key_live[:, :, None, :] & (key_pos[:, :, None, :] <= query_pos[:, None, :, None])
    visible = visible[:, :, None]
    masked = jnp.where(visible, scores, NEG)
    new_max = jnp.maximum(maxima, jnp.max(masked, axis=-1))
    decay_old = jnp.exp(maxima - new_max)
    probs = jnp.where(visible, jnp.exp(scores - new_max[..., None]), 0.0)
    totals = totals * decay_old + jnp.sum(probs, axis=-1)
    running = running * decay_old[..., None] + jnp.einsum(
        "bngqs,bnsd->bngqd",
        probs.astype(jnp.bfloat16),
        value_tiles,
        preferred_element_type=jnp.float32,
    )
    return (new_max, totals, running)


def attend(
    query_group,
    query_ids,
    key_table,
    value_table,
    slash_offsets,
    slash_counts,
    vertical_blocks,
    vertical_counts,
):
    group_count, block_len, local_groups, group_heads, head_dim = query_group.shape
    slash_list = jnp.transpose(slash_offsets[:, query_ids], (1, 0, 2))
    slash_live = jnp.transpose(slash_counts[:, query_ids])
    vertical_list = jnp.transpose(vertical_blocks[:, query_ids], (1, 0, 2))
    vertical_live = jnp.transpose(vertical_counts[:, query_ids])
    state_shape = (group_count, local_groups, group_heads, block_len)
    carry_state = (
        jnp.full(state_shape, NEG, jnp.float32),
        jnp.zeros(state_shape, jnp.float32),
        jnp.zeros(state_shape + (head_dim,), jnp.float32),
    )
    couple = jnp.arange(2, dtype=jnp.int32)

    def slash_step(turn, state_now):
        picked = lax.dynamic_slice_in_dim(slash_list, 2 * turn, 2, axis=2)
        blocks = query_ids[:, None, None] - picked
        live_slots = (2 * turn + couple)[None, None, :] < slash_live[:, :, None]
        return visit(state_now, query_group, key_table, value_table, query_ids, blocks, live_slots)

    def vertical_step(turn, state_now):
        blocks = lax.dynamic_slice_in_dim(vertical_list, 2 * turn, 2, axis=2)
        live_slots = (2 * turn + couple)[None, None, :] < vertical_live[:, :, None]
        return visit(state_now, query_group, key_table, value_table, query_ids, blocks, live_slots)

    carry_state = lax.fori_loop(0, (jnp.max(slash_live) + 1) // 2, slash_step, carry_state)
    carry_state = lax.fori_loop(0, (jnp.max(vertical_live) + 1) // 2, vertical_step, carry_state)
    maxima, totals, running = carry_state
    result = (running / totals[..., None]).astype(jnp.bfloat16)
    return jnp.transpose(result, (0, 3, 1, 2, 4)).reshape(
        group_count * block_len, local_groups * group_heads, head_dim
    )


def on_device(
    query_states,
    key_states,
    value_states,
    slash_offsets,
    slash_counts,
    vertical_blocks,
    vertical_counts,
):
    ctx_rank = lax.axis_index("ctx")
    query_local, key_local, value_local = (
        lax.all_to_all(query_states, "head", split_axis=1, concat_axis=0, tiled=True),
        lax.all_to_all(key_states, "head", split_axis=1, concat_axis=0, tiled=True),
        lax.all_to_all(value_states, "head", split_axis=1, concat_axis=0, tiled=True),
    )
    key_full, value_full = (
        lax.all_gather(key_local, "ctx", axis=0, tiled=True),
        lax.all_gather(value_local, "ctx", axis=0, tiled=True),
    )
    local_rows, heads_local, head_dim = query_local.shape
    local_groups = heads_local // G
    seq_blocks = key_full.shape[0] // BLK
    key_table = key_full.reshape(seq_blocks, BLK, local_groups, head_dim)
    value_table = value_full.reshape(seq_blocks, BLK, local_groups, head_dim)
    query_blocks = local_rows // BLK
    query_ids = ctx_rank * query_blocks + jnp.arange(query_blocks, dtype=jnp.int32)
    group_size = 512 // BLK
    group_total = query_blocks // group_size
    query_grouped = query_local.reshape(group_total, group_size, BLK, local_groups, G, head_dim)

    def run_group(entries):
        return attend(
            entries[0],
            entries[1],
            key_table,
            value_table,
            slash_offsets,
            slash_counts,
            vertical_blocks,
            vertical_counts,
        )

    answers = lax.map(run_group, (query_grouped, query_ids.reshape(group_total, group_size)))
    answers = answers.reshape(local_rows, heads_local, head_dim)
    return lax.all_to_all(answers, "head", split_axis=0, concat_axis=1, tiled=True)


def solution(mesh):
    in_specs = (
        P(("ctx", "head"), None, None),
        P(("ctx", "head"), None, None),
        P(("ctx", "head"), None, None),
        P("head", None, None),
        P("head", None),
        P("head", None, None),
        P("head", None),
    )
    out_specs = P(("ctx", "head"), None, None)
    return jax.shard_map(
        on_device, mesh=mesh, in_specs=in_specs, out_specs=out_specs, check_vma=False
    )
```

profile of v0, /device:TPU:96, one launch (start us, length us, event | category | flops | bytes accessed | tf_op | source)
XLA Modules:
  0.0 660.0 jit_solution(3249853632355213992)
XLA Ops:
  7.5 11.7 %all_to_all.69 = bf16[128,8,128]{2,0,1:T(8,128)(2,1)} all-to-all(bf16[128,8,128]{2,0,1:T(8,128)(2,1)S(1)} %copy.89), channel_id=1, replica_groups=mesh['ctx'=16,'head'=8] {'head'}, dimensions={1} | all-to-all | bytes 524288 | tf_op jit(solution)/shard_map/all_to_all | solution.py:101
  20.3 10.6 %all_to_all.70 = bf16[128,8,128]{2,0,1:T(8,128)(2,1)} all-to-all(bf16[128,8,128]{2,0,1:T(8,128)(2,1)S(1)} %copy.90), channel_id=1, replica_groups=mesh['ctx'=16,'head'=8] {'head'}, dimensions={1} | all-to-all | bytes 524288 | tf_op jit(solution)/shard_map/all_to_all | solution.py:102
  30.9 6.8 %copy.86 = bf16[128,128,128]{2,0,1:T(8,128)(2,1)} copy(bf16[128,128,128]{2,1,0:T(8,128)(2,1)} %param.13) | data formatting | bytes 8388608 | tf_op args[0]
  42.7 49.4 %all-to-all-done = bf16[128,128,128]{2,0,1:T(8,128)(2,1)} async-done(((bf16[128,128,128]{2,0,1:T(8,128)(2,1)}), bf16[128,128,128]{2,0,1:T(8,128)(2,1)}, u32[]{:S(2)}, u32[]{:S(2)}) %all-to-all-start) | async-done | bytes 4194336 | tf_op jit(solution)/shard_map/all_to_all | solution.py:100
  92.1 6.9 %copy.88 = bf16[8,128,16,128]{3,2,1,0:T(8,128)(2,1)} copy(bf16[8,128,16,128]{3,1,2,0:T(8,128)(2,1)} %bitcast.17) | data formatting | bytes 8388608 | tf_op jit(solution)/shard_map/all_to_all | solution.py:100
  99.0 24.4 %all-gather.5.cloned.1.call-done = bf16[16384,1,128]{2,0,1:T(8,128)(2,1)} async-done(((bf16[1024,1,128]{2,0,1:T(8,128)(2,1)}), bf16[16384,1,128]{2,0,1:T(8,128)(2,1)}) %all-gather.5.cloned.1.call-update) | async-done | bytes 4194320 | tf_op jit(solution)/shard_map/all_gather | solution.py:106
  123.4 472.6 %while.81 = (s32[]{:T(128)}, bf16[2,512,16,128]{3,2,1,0:T(8,128)(2,1)}, s32[2,8]{1,0:T(2,128)S(1)}, s32[1,256]{1,0:T(1,128)S(1)}, s32[1,256,12]{2,1,0:T(8,128)S(...) while((s32[]{:T(128)}, ...), condition=%wide.region_11.12_spmd, body=%wide.region_0.11_spmd.sunk | while | flops 1103417728 | bytes 111853656 | solution.py:131
  130.9 110.1 %while.82 = (s32[]{:T(128)}, f32[8,1,16,64]{3,2,0,1:T(8,128)S(1)}, f32[8,1,16,64]{3,2,0,1:T(8,128)S(1)}, f32[8,1,16,64,128]{4,3,2,0,1:T(8,128)}, s32[]{:T(128)},...) while((s32[]{:T(128)}, f32[8,1,16,64]{3,2,0,1:T(8,128)S(1)}, ...), condition=%wide.region_5.5_spmd.clone, body=%wide.region_2.4_spmd.clone.sunk | while | flops 550659776 | bytes 42241712 | solution.py:80
  140.7 6.1 bitcast_add_fusion.9
  177.4 6.1 bitcast_add_fusion.9
  195.7 6.1 bitcast_add_fusion.9
  232.4 6.1 bitcast_add_fusion.9
  243.6 110.1 %while.83 = (s32[]{:T(128)}, f32[8,1,16,64]{3,2,0,1:T(8,128)S(1)}, f32[8,1,16,64]{3,2,0,1:T(8,128)S(1)}, f32[8,1,16,64,128]{4,3,2,0,1:T(8,128)}, s32[]{:T(128)},...) while((s32[]{:T(128)}, f32[8,1,16,64]{3,2,0,1:T(8,128)S(1)}, ...), condition=%wide.region_10.10_spmd.clone, body=%wide.region_7.9_spmd.clone.sunk | while | flops 550659712 | bytes 42241680 | solution.py:81
  253.4 6.1 bitcast_add_fusion.11
  271.7 6.1 bitcast_add_fusion.11
  290.1 6.1 bitcast_add_fusion.11
  308.4 6.1 bitcast_add_fusion.11
  326.8 6.1 bitcast_add_fusion.11
  345.1 6.1 bitcast_add_fusion.11
  367.2 110.1 %while.82 = (s32[]{:T(128)}, f32[8,1,16,64]{3,2,0,1:T(8,128)S(1)}, f32[8,1,16,64]{3,2,0,1:T(8,128)S(1)}, f32[8,1,16,64,128]{4,3,2,0,1:T(8,128)}, s32[]{:T(128)},...) while((s32[]{:T(128)}, f32[8,1,16,64]{3,2,0,1:T(8,128)S(1)}, ...), condition=%wide.region_5.5_spmd.clone, body=%wide.region_2.4_spmd.clone.sunk | while | flops 550659776 | bytes 42241712 | solution.py:80
  395.3 6.1 bitcast_add_fusion.9
  413.7 6.1 bitcast_add_fusion.9
  450.4 6.1 bitcast_add_fusion.9
  468.7 6.1 bitcast_add_fusion.9
  479.9 110.1 %while.83 = (s32[]{:T(128)}, f32[8,1,16,64]{3,2,0,1:T(8,128)S(1)}, f32[8,1,16,64]{3,2,0,1:T(8,128)S(1)}, f32[8,1,16,64,128]{4,3,2,0,1:T(8,128)}, s32[]{:T(128)},...) while((s32[]{:T(128)}, f32[8,1,16,64]{3,2,0,1:T(8,128)S(1)}, ...), condition=%wide.region_10.10_spmd.clone, body=%wide.region_7.9_spmd.clone.sunk | while | flops 550659712 | bytes 42241680 | solution.py:81
  489.7 6.1 bitcast_add_fusion.11
  508.0 6.1 bitcast_add_fusion.11
  526.4 6.1 bitcast_add_fusion.11
  544.7 6.1 bitcast_add_fusion.11
  563.1 6.1 bitcast_add_fusion.11
  581.4 6.1 bitcast_add_fusion.11
  596.0 53.9 %all_to_all.71 = bf16[1024,16,128]{2,1,0:T(8,128)(2,1)S(1)} all-to-all(bf16[1024,16,128]{2,1,0:T(8,128)(2,1)} %bitcast.29), channel_id=1, replica_groups=mesh['ctx'=16,'head'=8] {'head'}, dimensions={0} | all-to-all | bytes 8388608 | tf_op jit(solution)/shard_map/all_to_all | solution.py:133
  (711 shorter events, 355.8 us)
Async XLA Ops:
  6.5 92.5 %all-gather.3.cloned.1.call-start = ((), (), s32[]{:S(2)}) async-start(), calls=%async_computation.4 | async-start | bytes 4456448 | tf_op jit(solution)/shard_map/all_gather | solution.py:105
  19.3 104.1 %all-gather.5.cloned.1.call-start = ((), (), s32[]{:S(2)}) async-start(), calls=%async_computation.5 | async-start | bytes 4456448 | tf_op jit(solution)/shard_map/all_gather | solution.py:106
  37.7 4.7 copy-start.4
  37.7 4.9 copy-start.5
  37.7 54.4 %all-to-all-start = ((bf16[128,128,128]{2,0,1:T(8,128)(2,1)}), bf16[128,128,128]{2,0,1:T(8,128)(2,1)}, u32[]{:S(2)}, u32[]{:S(2)}) async-start(bf16[128,128,128]{2,0,1:T(8,128)(2,1)} %copy.86), calls=%async_computation | async-start | bytes 8388608 | tf_op jit(solution)/shard_map/all_to_all | solution.py:100
  92.1 31.3 %copy-start.2 = (s32[1,256]{1,0:T(1,128)S(1)}, s32[1,256]{1,0:T(1,128)}, u32[]{:S(2)}) copy-start(s32[1,256]{1,0:T(1,128)} %param.17) | copy-start | bytes 3076
  92.1 31.3 %copy-start.3 = (s32[1,256]{1,0:T(1,128)S(1)}, s32[1,256]{1,0:T(1,128)}, u32[]{:S(2)}) copy-start(s32[1,256]{1,0:T(1,128)} %param.19) | copy-start | bytes 3076
  140.7 6.1 copy-start
  159.0 6.1 copy-start
  177.4 6.1 copy-start
  195.7 6.1 copy-start
  214.1 6.1 copy-start
  232.4 6.1 copy-start
  253.4 6.1 copy-start.1
  271.7 6.1 copy-start.1
  290.1 6.1 copy-start.1
  308.4 6.1 copy-start.1
  326.8 6.1 copy-start.1
  345.1 6.1 copy-start.1
  376.9 6.1 copy-start
  395.3 6.1 copy-start
  413.7 6.1 copy-start
  432.0 6.1 copy-start
  450.4 6.1 copy-start
  468.7 6.1 copy-start
  489.7 6.1 copy-start.1
  508.0 6.1 copy-start.1
  526.4 6.1 copy-start.1
  544.7 6.1 copy-start.1
  563.1 6.1 copy-start.1
  581.4 6.1 copy-start.1
Sparse Core Ops, SparseCore 0:
  19.4 50.7 all-gather.2
  72.3 51.0 all-gather.4
where the time goes:
time: 662 us; the launch traced here: 660 us
  matrix products  222 us (34%)
  local copies, waits for them, and re-layouts  190 us (29%)
  blocking collectives  76.2 us (12%)
  other arithmetic  74.9 us (11%)
  waiting for transfers between devices  73.8 us (11%)
  between operations  13.4 us (2%)
    dot_general x24, matrix products, visit(): jnp.einsum('bngqs,bnsd->bngqd', probs.astype(jnp.bfloat16), value_tiles,...  147 us
    dot_general x24, matrix products, visit(): jnp.einsum('bqngd,bnsd->bngqs', query_group, key_tiles, preferred_element...  75.1 us
    gather x24, local copies, waits for them, and re-layouts, visit(): key_table[blocks, :, head_lanes]  66.9 us
    gather x24, local copies, waits for them, and re-layouts, visit(): value_table[blocks, :, head_lanes]  66.9 us
    reduce_sum x24, other arithmetic, visit(): totals = totals * decay_old + jnp.sum(probs, axis=-1)  57.2 us
    all_to_all x1, blocking collectives, on_device(): lax.all_to_all(answers, 'head', split_axis=0, concat_axis=1, tiled=True)  53.9 us
    all_to_all x1, waiting for transfers between devices, on_device(): lax.all_to_all(query_states, 'head', split_axis=1, concat_axis=0, tiled=T...  49.4 us
    all_gather x1, waiting for transfers between devices, on_device(): lax.all_gather(value_local, 'ctx', axis=0, tiled=True)  24.4 us
  transfers between devices with their start and end apart: 3, of which 2 were waited for; matrix products, arithmetic and copies ran while one was open for 2% of the time, Pallas kernels for 0%

commit v1 on v0

--- a/solution.py
+++ b/solution.py
@@ -103,7 +103,9 @@
     )
     key_full, value_full = (
         lax.all_gather(key_local, "ctx", axis=0, tiled=True),
-        lax.all_gather(value_local, "ctx", axis=0, tiled=True),
+        jnp.concatenate(
+            lax.all_to_all(jnp.stack([value_local] * lax.axis_size("ctx")), "ctx", 0, 0), axis=0
+        ),
     )
     local_rows, heads_local, head_dim = query_local.shape
     local_groups = heads_local // G

time: 662 us -> 696 us (1.051)
  blocking collectives: 76.2 us -> 119 us
  waiting for transfers between devices: 73.8 us -> 54.6 us
    all_to_all x1, blocking collectives: 10.6 us -> 54.2 us  [on_device(): lax.all_to_all(query_states, 'head', split_axis=1, concat_axis=0, tiled=T...]
    all_gather x1 -> x0, waiting for transfers between devices: 24.4 us -> none  [on_device(): lax.all_gather(value_local, 'ctx', axis=0, tiled=True)]
    all_to_all x1 -> x2, waiting for transfers between devices: 49.4 us -> 54.6 us  [the longest x1 54.1 us: on_device(): lax.all_to_all(jnp.stack([value_local] * lax.axis_size('ctx')), 'ctx', 0, 0)]
  transfers between devices with their start and end apart: 3 -> 3, of which waited for: 2 -> 2; matrix products, arithmetic and copies ran while one was open for 2% -> 3% of each run, Pallas kernels for 0% -> 0%
where the time goes in v1:
time: 696 us; the launch traced here: 693 us
  matrix products  222 us (32%)
  local copies, waits for them, and re-layouts  194 us (28%)
  blocking collectives  119 us (17%)
  other arithmetic  75 us (11%)
  waiting for transfers between devices  54.6 us (8%)
  between operations  13.4 us (2%)
  starting transfers between devices  10.7 us (2%)
    dot_general x24, matrix products, visit(): jnp.einsum('bngqs,bnsd->bngqd', probs.astype(jnp.bfloat16), value_tiles,...  146 us
    dot_general x24, matrix products, visit(): jnp.einsum('bqngd,bnsd->bngqs', query_group, key_tiles, preferred_element...  75.2 us
    gather x24, local copies, waits for them, and re-layouts, visit(): key_table[blocks, :, head_lanes]  66.9 us
    gather x24, local copies, waits for them, and re-layouts, visit(): value_table[blocks, :, head_lanes]  66.9 us
    reduce_sum x24, other arithmetic, visit(): totals = totals * decay_old + jnp.sum(probs, axis=-1)  57.2 us
    all_to_all x1, blocking collectives, on_device(): lax.all_to_all(query_states, 'head', split_axis=1, concat_axis=0, tiled=T...  54.2 us
    all_to_all x1, waiting for transfers between devices, on_device(): lax.all_to_all(jnp.stack([value_local] * lax.axis_size('ctx')), 'ctx', 0, 0)  54.1 us
    all_to_all x1, blocking collectives, on_device(): lax.all_to_all(answers, 'head', split_axis=0, concat_axis=1, tiled=True)  53.3 us
  transfers between devices with their start and end apart: 3, of which 2 were waited for; matrix products, arithmetic and copies ran while one was open for 3% of the time, Pallas kernels for 0%

profile of v1, /device:TPU:96, one launch (start us, length us, event | category | flops | bytes accessed | tf_op | source)
XLA Modules:
  0.0 693.4 jit_solution(9896173245592337633)
XLA Ops:
  7.5 11.7 %all_to_all.71 = bf16[128,8,128]{2,0,1:T(8,128)(2,1)} all-to-all(bf16[128,8,128]{2,0,1:T(8,128)(2,1)S(1)} %copy.89), channel_id=1, replica_groups=mesh['ctx'=16,'head'=8] {'head'}, dimensions={1} | all-to-all | bytes 524288 | tf_op jit(solution)/shard_map/all_to_all | solution.py:101
  24.4 6.9 copy.86
  31.8 54.2 %all_to_all.72 = bf16[128,128,128]{2,0,1:T(8,128)(2,1)} all-to-all(bf16[128,128,128]{2,0,1:T(8,128)(2,1)} %copy.86), channel_id=1, replica_groups=mesh['ctx'=16,'head'=8] {'head'}, dimensions={1} | all-to-all | bytes 8388608 | tf_op jit(solution)/shard_map/all_to_all | solution.py:100
  88.7 7.3 %all-to-all-start.3 = ((bf16[16,1024,1,128]{3,1,2,0:T(8,128)(2,1)}), bf16[16,1024,1,128]{3,1,2,0:T(8,128)(2,1)}, u32[]{:S(2)}, u32[]{:S(2)}) async-start(bf16[16,1024,1,128]{3,1,2,0:T(8,128)(2,1)} %stack.5), calls=%async_computation.3 | async-start | bytes 8388608 | tf_op jit(solution)/shard_map/all_to_all | solution.py:107
  96.3 6.8 copy.88
  103.1 54.1 %all-to-all-done.3 = bf16[16,1024,1,128]{3,1,2,0:T(8,128)(2,1)} async-done(((bf16[16,1024,1,128]{3,1,2,0:T(8,128)(2,1)}), bf16[16,1024,1,128]{3,1,2,0:T(8,128)(2,1)}, u32[]{:S(2)}, u32[]{:S(2)}) %all-to-all-start.3) | async-done | bytes 4194336 | tf_op jit(solution)/shard_map/all_to_all | solution.py:107
  157.2 472.8 %while.81 = (s32[]{:T(128)}, bf16[2,512,16,128]{3,2,1,0:T(8,128)(2,1)}, s32[2,8]{1,0:T(2,128)S(1)}, s32[1,256]{1,0:T(1,128)S(1)}, s32[1,256,12]{2,1,0:T(8,128)S(...) while((s32[]{:T(128)}, ...), condition=%wide.region_11.12_spmd, body=%wide.region_0.11_spmd.sunk | while | flops 1103417728 | bytes 111853656 | solution.py:133
  165.0 110.1 %while.82 = (s32[]{:T(128)}, f32[8,1,16,64]{3,2,0,1:T(8,128)S(1)}, f32[8,1,16,64]{3,2,0,1:T(8,128)S(1)}, f32[8,1,16,64,128]{4,3,2,0,1:T(8,128)}, s32[]{:T(128)},...) while((s32[]{:T(128)}, f32[8,1,16,64]{3,2,0,1:T(8,128)S(1)}, ...), condition=%wide.region_5.5_spmd.clone, body=%wide.region_2.4_spmd.clone.sunk | while | flops 550659776 | bytes 42241712 | solution.py:80
  174.8 6.1 bitcast_add_fusion.9
  193.2 6.1 bitcast_add_fusion.9
  211.5 6.1 bitcast_add_fusion.9
  229.9 6.1 bitcast_add_fusion.9
  248.2 6.1 bitcast_add_fusion.9
  266.6 6.1 bitcast_add_fusion.9
  277.7 110.0 %while.83 = (s32[]{:T(128)}, f32[8,1,16,64]{3,2,0,1:T(8,128)S(1)}, f32[8,1,16,64]{3,2,0,1:T(8,128)S(1)}, f32[8,1,16,64,128]{4,3,2,0,1:T(8,128)}, s32[]{:T(128)},...) while((s32[]{:T(128)}, f32[8,1,16,64]{3,2,0,1:T(8,128)S(1)}, ...), condition=%wide.region_10.10_spmd.clone, body=%wide.region_7.9_spmd.clone.sunk | while | flops 550659712 | bytes 42241680 | solution.py:81
  287.5 6.1 bitcast_add_fusion.11
  305.8 6.1 bitcast_add_fusion.11
  324.2 6.1 bitcast_add_fusion.11
  360.9 6.1 bitcast_add_fusion.11
  379.2 6.1 bitcast_add_fusion.11
  401.3 110.1 %while.82 = (s32[]{:T(128)}, f32[8,1,16,64]{3,2,0,1:T(8,128)S(1)}, f32[8,1,16,64]{3,2,0,1:T(8,128)S(1)}, f32[8,1,16,64,128]{4,3,2,0,1:T(8,128)}, s32[]{:T(128)},...) while((s32[]{:T(128)}, f32[8,1,16,64]{3,2,0,1:T(8,128)S(1)}, ...), condition=%wide.region_5.5_spmd.clone, body=%wide.region_2.4_spmd.clone.sunk | while | flops 550659776 | bytes 42241712 | solution.py:80
  411.1 6.1 bitcast_add_fusion.9
  447.8 6.1 bitcast_add_fusion.9
  466.2 6.1 bitcast_add_fusion.9
  484.5 6.1 bitcast_add_fusion.9
  502.9 6.1 bitcast_add_fusion.9
  514.0 110.0 %while.83 = (s32[]{:T(128)}, f32[8,1,16,64]{3,2,0,1:T(8,128)S(1)}, f32[8,1,16,64]{3,2,0,1:T(8,128)S(1)}, f32[8,1,16,64,128]{4,3,2,0,1:T(8,128)}, s32[]{:T(128)},...) while((s32[]{:T(128)}, f32[8,1,16,64]{3,2,0,1:T(8,128)S(1)}, ...), condition=%wide.region_10.10_spmd.clone, body=%wide.region_7.9_spmd.clone.sunk | while | flops 550659712 | bytes 42241680 | solution.py:81
  523.8 6.1 bitcast_add_fusion.11
  542.1 6.1 bitcast_add_fusion.11
  578.8 6.1 bitcast_add_fusion.11
  615.5 6.1 bitcast_add_fusion.11
  630.1 53.3 %all_to_all.73 = bf16[1024,16,128]{2,1,0:T(8,128)(2,1)S(1)} all-to-all(bf16[1024,16,128]{2,1,0:T(8,128)(2,1)} %bitcast.29), channel_id=1, replica_groups=mesh['ctx'=16,'head'=8] {'head'}, dimensions={0} | all-to-all | bytes 8388608 | tf_op jit(solution)/shard_map/all_to_all | solution.py:135
  (711 shorter events, 358.5 us)
Async XLA Ops:
  6.5 150.7 %all-gather.2.cloned.1.call-start = ((), (), s32[]{:S(2)}) async-start(), calls=%async_computation.5 | async-start | bytes 4456448 | tf_op jit(solution)/shard_map/all_gather | solution.py:105
  20.9 10.8 %all-to-all-start.2 = ((bf16[128,8,128]{2,0,1:T(8,128)(2,1)}), bf16[128,8,128]{2,0,1:T(8,128)(2,1)S(1)}, u32[]{:S(2)}, u32[]{:S(2)}) async-start(bf16[128,8,128]{2,0,1:T(8,128)(2,1)} %copy.90), calls=%async_computation.2 | async-start | bytes 524288 | tf_op jit(solution)/shard_map/all_to_all | solution.py:102
  88.7 7.3 %copy-start.4 = (s32[1,256,12]{1,0,2:T(1,128)S(1)}, s32[1,256,12]{1,0,2:T(1,128)}, u32[]{:S(2)}) copy-start(s32[1,256,12]{1,0,2:T(1,128)} %param.16) | copy-start | bytes 36868
  88.7 7.4 %copy-start.5 = (s32[1,256,12]{1,0,2:T(1,128)S(1)}, s32[1,256,12]{1,0,2:T(1,128)}, u32[]{:S(2)}) copy-start(s32[1,256,12]{1,0,2:T(1,128)} %param.18) | copy-start | bytes 36868
  88.7 68.5 %all-to-all-start.3 = ((bf16[16,1024,1,128]{3,1,2,0:T(8,128)(2,1)}), bf16[16,1024,1,128]{3,1,2,0:T(8,128)(2,1)}, u32[]{:S(2)}, u32[]{:S(2)}) async-start(bf16[16,1024,1,128]{3,1,2,0:T(8,128)(2,1)} %stack.5), calls=%async_computation.3 | async-start | bytes 8388608 | tf_op jit(solution)/shard_map/all_to_all | solution.py:107
  96.3 61.0 %copy-start.2 = (s32[1,256]{1,0:T(1,128)S(1)}, s32[1,256]{1,0:T(1,128)}, u32[]{:S(2)}) copy-start(s32[1,256]{1,0:T(1,128)} %param.17) | copy-start | bytes 3076
  96.3 61.0 %copy-start.3 = (s32[1,256]{1,0:T(1,128)S(1)}, s32[1,256]{1,0:T(1,128)}, u32[]{:S(2)}) copy-start(s32[1,256]{1,0:T(1,128)} %param.19) | copy-start | bytes 3076
  174.8 6.1 copy-start
  193.2 6.1 copy-start
  211.5 6.1 copy-start
  229.9 6.1 copy-start
  248.2 6.1 copy-start
  266.6 6.1 copy-start
  287.5 6.1 copy-start.1
  305.8 6.1 copy-start.1
  324.2 6.1 copy-start.1
  342.5 6.1 copy-start.1
  360.9 6.1 copy-start.1
  379.2 6.1 copy-start.1
  411.1 6.1 copy-start
  429.5 6.1 copy-start
  447.8 6.1 copy-start
  466.2 6.1 copy-start
  484.5 6.1 copy-start
  502.9 6.1 copy-start
  523.8 6.1 copy-start.1
  542.1 6.1 copy-start.1
  560.5 6.1 copy-start.1
  578.8 6.1 copy-start.1
  597.2 6.1 copy-start.1
  615.5 6.1 copy-start.1
Sparse Core Ops, SparseCore 0:
  19.4 50.7 all-gather.1
